TPU v7x, 32 devices: a whole 2x2x4 slice. The times are simulated.
32 devices in a mesh: dp: 4 (over y, x), sp: 8 (over z, core).
Axes of the slice: x: 2, y: 2, z: 4, core: 2. Of those that a mesh axis runs over, the one named last changes fastest.
Arguments:
- tokens: bfloat16 [32768, 1024], P(('dp', 'sp')), may hold values from -6 to 6
- doc_ids: int32 [4, 8192], P('dp'), may hold values from 0 to 15, never falling along the last dimension, each value on 1 to 4096 neighbouring positions
- gain_attn: bfloat16 [1024], P('sp'), may hold values from 0.5 to 1.5
- w_query: bfloat16 [1024, 256], P('sp'), may hold values from -0.1875 to 0.1875
- w_key: bfloat16 [1024, 256], P('sp'), may hold values from -0.1875 to 0.1875
- w_value: bfloat16 [1024, 1024], P('sp'), may hold values from -0.1875 to 0.1875
- w_out: bfloat16 [1024, 1024], P(None, 'sp'), may hold values from -2 to 2
- gain_mlp: bfloat16 [1024], P('sp'), may hold values from 0.5 to 1.5
- w_gate: bfloat16 [1024, 2752], P('sp'), may hold values from -0.1875 to 0.1875
- w_up: bfloat16 [1024, 2752], P('sp'), may hold values from -0.1875 to 0.1875
- w_down: bfloat16 [2752, 1024], P(None, 'sp'), may hold values from -0.109375 to 0.109375
- cotangent: bfloat16 [32768, 1024], P(('dp', 'sp')), may hold values from -6 to 6
Outputs:
- output: bfloat16 [32768, 1024], P(('dp', 'sp'))
- grad_input: float32 [32768, 1024], P(('dp', 'sp'))
- grad_gain_attn: float32 [1024], P('sp')
- grad_query: float32 [1024, 256], P('sp')
- grad_key: float32 [1024, 256], P('sp')
- grad_value: float32 [1024, 1024], P('sp')
- grad_out: float32 [1024, 1024], P(None, 'sp')
- grad_gain_mlp: float32 [1024], P('sp')
- grad_gate: float32 [1024, 2752], P('sp')
- grad_up: float32 [1024, 2752], P('sp')
- grad_down: float32 [2752, 1024], P(None, 'sp')
Inputs may be any that keep to these rules, and one draw needn't show every extreme that they name: `doc_ids`: within each group document numbers never fall along the tokens, every number 0 to 15 is used, each document has 1 to 4096 tokens and one has exactly 4096.
All inputs are finite; a program needn't handle non-finite values.
Results may differ from a plain program's by a relative error of at most 0.019.
Values may be sent and summed in bfloat16 or wider, within the bound.
A program may use at most 192 MiB of HBM per device.

v0:
```python
import math
import jax
import jax.numpy as jnp
from jax import lax
from jax.sharding import PartitionSpec as P

FEAT = 16
HEAD_V = 64
BLOCK = 512
EPSILON = 1e-05
CAREFUL = lax.Precision.HIGH


def rms_scale(values, weights):
    return values * lax.rsqrt(jnp.mean(values * values, axis=-1, keepdims=True) + EPSILON) * weights


def taylor(vectors):
    feature_dim = vectors.shape[-1]
    scale_one = 1.0 / math.sqrt(math.sqrt(feature_dim))
    scale_two = 1.0 / (math.sqrt(2.0) * math.sqrt(feature_dim))
    products = (vectors[..., :, None] * vectors[..., None, :]).reshape(
        vectors.shape[:-1] + (feature_dim * feature_dim,)
    )
    return jnp.concatenate(
        [
            jnp.ones(vectors.shape[:-1] + (1,), vectors.dtype),
            vectors * scale_one,
            products * scale_two,
        ],
        axis=-1,
    )


def attend_block(carried, blocks):
    kv_state, key_total, last_doc = carried
    query_blk, key_blk, value_blk, doc_blk = blocks
    feature_dim = query_blk.shape[-1]
    length_blk = doc_blk.shape[0]
    scores = jnp.einsum("hif,hjf->hij", query_blk, key_blk, precision=CAREFUL)
    position = lax.iota(jnp.int32, length_blk)
    allowed = (position[:, None] >= position[None, :]) & (doc_blk[:, None] == doc_blk[None, :])
    weights = jnp.where(
        allowed[None],
        1.0 + scores / math.sqrt(feature_dim) + scores * scores / (2.0 * feature_dim),
        0.0,
    )
    query_map = taylor(query_blk)
    key_map = taylor(key_blk)
    sees_prior = (doc_blk == last_doc).astype(query_blk.dtype)
    numerator = jnp.einsum("hij,hjv->hiv", weights, value_blk, precision=CAREFUL) + sees_prior[
        None, :, None
    ] * jnp.einsum("hif,hfv->hiv", query_map, kv_state, precision=CAREFUL)
    denominator = jnp.sum(weights, axis=-1) + sees_prior[None, :] * jnp.einsum(
        "hif,hf->hi", query_map, key_total, precision=CAREFUL
    )
    attended = numerator / denominator[..., None]
    tail_doc = doc_blk[length_blk - 1]
    keep_old = (tail_doc == last_doc).astype(query_blk.dtype)
    in_tail = (doc_blk == tail_doc).astype(query_blk.dtype)
    key_tail = key_map * in_tail[None, :, None]
    kv_state = keep_old * kv_state + jnp.einsum(
        "hjf,hjv->hfv", key_tail, value_blk, precision=CAREFUL
    )
    key_total = keep_old * key_total + jnp.sum(key_tail, axis=1)
    return ((kv_state, key_total, tail_doc), attended)


def attend(queries, keys_in, values_in, doc_row):
    head_count, feature_dim, length = queries.shape
    value_dim = values_in.shape[1]
    block_count = length // BLOCK
    mapped_dim = 1 + feature_dim + feature_dim * feature_dim

    def blocked(tensor):
        inner_dim = tensor.shape[1]
        return tensor.reshape(head_count, inner_dim, block_count, BLOCK).transpose(2, 0, 3, 1)

    initial = (
        jnp.zeros((head_count, mapped_dim, value_dim), queries.dtype),
        jnp.zeros((head_count, mapped_dim), queries.dtype),
        jnp.array(-1, jnp.int32),
    )
    _, outputs = lax.scan(
        jax.checkpoint(attend_block),
        initial,
        (
            blocked(queries),
            blocked(keys_in),
            blocked(values_in),
            doc_row.reshape(block_count, BLOCK),
        ),
    )
    return outputs.transpose(1, 3, 0, 2).reshape(head_count, value_dim, length)


def joined(query_w, key_w, value_w):
    model_dim = query_w.shape[0]
    head_count = query_w.shape[1] // FEAT
    stacked = jnp.concatenate(
        [
            query_w.reshape(model_dim, head_count, FEAT),
            key_w.reshape(model_dim, head_count, FEAT),
            value_w.reshape(model_dim, head_count, HEAD_V),
        ],
        axis=2,
    )
    return stacked.reshape(model_dim, head_count * (2 * FEAT + HEAD_V))


def body(
    tokens,
    doc_ids,
    gain_attn,
    w_query,
    w_key,
    w_value,
    w_out,
    gain_mlp,
    w_gate,
    w_up,
    w_down,
    cotangent,
):
    head_count = w_query.shape[1] // FEAT
    shard_sp = lax.axis_size("sp")
    heads_here = head_count // shard_sp
    per_head = 2 * FEAT + HEAD_V
    tok_local = tokens.shape[0]
    contract_first = (((0,), (0,)), ((), ()))
    attn_full = (
        lax.all_gather(gain_attn, "sp", axis=0, tiled=True),
        lax.all_gather(w_query, "sp", axis=0, tiled=True),
        lax.all_gather(w_key, "sp", axis=0, tiled=True),
        lax.all_gather(w_value, "sp", axis=0, tiled=True),
        lax.all_gather(w_out, "sp", axis=1, tiled=True),
    )
    mlp_full = (
        lax.all_gather(gain_mlp, "sp", axis=0, tiled=True),
        lax.all_gather(w_gate, "sp", axis=0, tiled=True),
        lax.all_gather(w_up, "sp", axis=0, tiled=True),
        lax.all_gather(w_down, "sp", axis=1, tiled=True),
    )
    resid = tokens.astype(jnp.float32)
    gain_one = attn_full[0].astype(jnp.float32)
    w_joint = joined(attn_full[1], attn_full[2], attn_full[3])
    model_dim = w_joint.shape[0]
    normed_one = rms_scale(resid, gain_one).astype(jnp.bfloat16)
    projected = lax.dot_general(
        w_joint, normed_one, (((0,), (1,)), ((), ())), preferred_element_type=jnp.float32
    ).astype(jnp.bfloat16)
    by_head = lax.all_to_all(
        projected.reshape(head_count, per_head, tok_local),
        "sp",
        split_axis=0,
        concat_axis=2,
        tiled=True,
    )
    head_rows = by_head.astype(jnp.float32)
    doc_row = doc_ids[0]

    def local_attention(queries, keys_in, values_in):
        return attend(queries, keys_in, values_in, doc_row)

    attended, attention_back = jax.vjp(
        local_attention,
        head_rows[:, :FEAT],
        head_rows[:, FEAT : 2 * FEAT],
        head_rows[:, 2 * FEAT :],
    )
    attended_rows = attended.astype(jnp.bfloat16).reshape(heads_here * HEAD_V, attended.shape[2])
    token_heads = lax.all_to_all(attended_rows, "sp", split_axis=1, concat_axis=0, tiled=True)
    branch = lax.dot_general(
        token_heads, attn_full[4], contract_first, preferred_element_type=jnp.float32
    )
    hidden = resid + branch
    gain_two = mlp_full[0].astype(jnp.float32)
    normed_two = rms_scale(hidden, gain_two).astype(jnp.bfloat16)
    gate = jnp.dot(normed_two, mlp_full[1], preferred_element_type=jnp.float32)
    up_proj = jnp.dot(normed_two, mlp_full[2], preferred_element_type=jnp.float32)
    sigmoid_gate = jax.nn.sigmoid(gate)
    mixed = (gate * sigmoid_gate * up_proj).astype(jnp.bfloat16)
    output = (hidden + jnp.dot(mixed, mlp_full[3], preferred_element_type=jnp.float32)).astype(
        jnp.bfloat16
    )
    fetched = (
        lax.all_gather(gain_attn, "sp", axis=0, tiled=True),
        lax.all_gather(w_query, "sp", axis=0, tiled=True),
        lax.all_gather(w_key, "sp", axis=0, tiled=True),
        lax.all_gather(w_value, "sp", axis=0, tiled=True),
        lax.all_gather(w_out, "sp", axis=1, tiled=True),
        lax.all_gather(gain_mlp, "sp", axis=0, tiled=True),
        lax.all_gather(w_gate, "sp", axis=0, tiled=True),
        lax.all_gather(w_up, "sp", axis=0, tiled=True),
        lax.all_gather(w_down, "sp", axis=1, tiled=True),
    )
    out_back = fetched[4]
    gate_back = fetched[6]
    up_back = fetched[7]
    down_back = fetched[8]
    joint_back = joined(fetched[1], fetched[2], fetched[3])
    grad_top = cotangent.astype(jnp.float32)
    grad_down = lax.dot_general(
        mixed, cotangent, contract_first, preferred_element_type=jnp.float32
    )
    grad_mixed = lax.dot_general(
        cotangent, down_back, (((1,), (1,)), ((), ())), preferred_element_type=jnp.float32
    )
    grad_gate_in = (
        grad_mixed * up_proj * sigmoid_gate * (1.0 + gate * (1.0 - sigmoid_gate))
    ).astype(jnp.bfloat16)
    grad_up_in = (grad_mixed * gate * sigmoid_gate).astype(jnp.bfloat16)
    grad_gate = lax.dot_general(
        normed_two, grad_gate_in, contract_first, preferred_element_type=jnp.float32
    )
    grad_up = lax.dot_general(
        normed_two, grad_up_in, contract_first, preferred_element_type=jnp.float32
    )
    grad_normed_two = lax.dot_general(
        grad_gate_in, gate_back, (((1,), (1,)), ((), ())), preferred_element_type=jnp.float32
    ) + lax.dot_general(
        grad_up_in, up_back, (((1,), (1,)), ((), ())), preferred_element_type=jnp.float32
    )
    _, norm_two_back = jax.vjp(rms_scale, hidden, gain_two)
    grad_hidden_part, grad_gain_two = norm_two_back(grad_normed_two)
    grad_hidden = grad_top + grad_hidden_part
    grad_branch = grad_hidden.astype(jnp.bfloat16)
    grad_out = jnp.dot(token_heads, grad_branch, preferred_element_type=jnp.float32)
    grad_attended = lax.dot_general(
        out_back, grad_branch, (((1,), (1,)), ((), ())), preferred_element_type=jnp.float32
    ).astype(jnp.bfloat16)
    grad_heads = lax.all_to_all(grad_attended, "sp", split_axis=0, concat_axis=1, tiled=True)
    grad_q, grad_k, grad_v = attention_back(
        grad_heads.astype(jnp.float32).reshape(heads_here, HEAD_V, grad_heads.shape[1])
    )
    grad_stack = jnp.concatenate([grad_q, grad_k, grad_v], axis=1).astype(jnp.bfloat16)
    grad_proj = lax.all_to_all(grad_stack, "sp", split_axis=2, concat_axis=0, tiled=True).reshape(
        head_count * per_head, tok_local
    )
    grad_joint = lax.dot_general(
        normed_one, grad_proj, (((0,), (1,)), ((), ())), preferred_element_type=jnp.float32
    ).reshape(model_dim, head_count, per_head)
    grad_query = grad_joint[:, :, :FEAT].reshape(model_dim, head_count * FEAT)
    grad_key = grad_joint[:, :, FEAT : 2 * FEAT].reshape(model_dim, head_count * FEAT)
    grad_value = grad_joint[:, :, 2 * FEAT :].reshape(model_dim, head_count * HEAD_V)
    grad_normed_one = lax.dot_general(
        grad_proj, joint_back, (((0,), (1,)), ((), ())), preferred_element_type=jnp.float32
    )
    _, norm_one_back = jax.vjp(rms_scale, resid, gain_one)
    grad_input_part, grad_gain_one = norm_one_back(grad_normed_one)
    grad_input = grad_hidden + grad_input_part
    shards = (
        lax.psum_scatter(
            grad_gain_one.astype(jnp.bfloat16), "sp", scatter_dimension=0, tiled=True
        ).astype(jnp.float32),
        lax.psum_scatter(
            grad_query.astype(jnp.bfloat16), "sp", scatter_dimension=0, tiled=True
        ).astype(jnp.float32),
        lax.psum_scatter(
            grad_key.astype(jnp.bfloat16), "sp", scatter_dimension=0, tiled=True
        ).astype(jnp.float32),
        lax.psum_scatter(
            grad_value.astype(jnp.bfloat16), "sp", scatter_dimension=0, tiled=True
        ).astype(jnp.float32),
        lax.psum_scatter(
            grad_out.astype(jnp.bfloat16), "sp", scatter_dimension=1, tiled=True
        ).astype(jnp.float32),
        lax.psum_scatter(
            grad_gain_two.astype(jnp.bfloat16), "sp", scatter_dimension=0, tiled=True
        ).astype(jnp.float32),
        lax.psum_scatter(
            grad_gate.astype(jnp.bfloat16), "sp", scatter_dimension=0, tiled=True
        ).astype(jnp.float32),
        lax.psum_scatter(
            grad_up.astype(jnp.bfloat16), "sp", scatter_dimension=0, tiled=True
        ).astype(jnp.float32),
        lax.psum_scatter(
            grad_down.astype(jnp.bfloat16), "sp", scatter_dimension=1, tiled=True
        ).astype(jnp.float32),
    )
    summed = (
        lax.psum(shards[0].astype(jnp.bfloat16), "dp").astype(jnp.float32),
        lax.psum(shards[1].astype(jnp.bfloat16), "dp").astype(jnp.float32),
        lax.psum(shards[2].astype(jnp.bfloat16), "dp").astype(jnp.float32),
        lax.psum(shards[3].astype(jnp.bfloat16), "dp").astype(jnp.float32),
        lax.psum(shards[4].astype(jnp.bfloat16), "dp").astype(jnp.float32),
        lax.psum(shards[5].astype(jnp.bfloat16), "dp").astype(jnp.float32),
        lax.psum(shards[6].astype(jnp.bfloat16), "dp").astype(jnp.float32),
        lax.psum(shards[7].astype(jnp.bfloat16), "dp").astype(jnp.float32),
        lax.psum(shards[8].astype(jnp.bfloat16), "dp").astype(jnp.float32),
    )
    return (
        output,
        grad_input,
        summed[0],
        summed[1],
        summed[2],
        summed[3],
        summed[4],
        summed[5],
        summed[6],
        summed[7],
        summed[8],
    )


def solution(mesh):
    placed = (
        P(("dp", "sp"), None),
        P("dp", None),
        P("sp"),
        P("sp", None),
        P("sp", None),
        P("sp", None),
        P(None, "sp"),
        P("sp"),
        P("sp", None),
        P("sp", None),
        P(None, "sp"),
        P(("dp", "sp"), None),
    )
    return jax.shard_map(
        body,
        mesh=mesh,
        in_specs=placed,
        out_specs=(
            P(("dp", "sp"), None),
            P(("dp", "sp"), None),
            P("sp"),
            P("sp", None),
            P("sp", None),
            P("sp", None),
            P(None, "sp"),
            P("sp"),
            P("sp", None),
            P("sp", None),
            P(None, "sp"),
        ),
        check_vma=False,
    )
```

profile of v0, /device:TPU:0, one launch (start us, length us, event | category | flops | bytes accessed | tf_op | source)
XLA Modules:
  0.0 1510.6 jit_solution(1957601974484054943)
XLA Ops:
  14.1 13.4 all-gather
  28.8 16.1 %all_gather.34 = bf16[1024,256]{0,1:T(8,128)(2,1)S(1)} all-gather(bf16[128,256]{0,1:T(8,128)(2,1)S(1)} %copy.123), channel_id=1, replica_groups=mesh['dp'=4,'sp'=8] {'sp'}, dimensions={0}, use_global_device_ids=true | all-gather | bytes 589824 | tf_op jit(solution)/shard_map/all_gather | solution.py:133
  45.0 13.9 all_gather.35
  60.9 5.0 convolution_convert_fusion.3
  65.9 4.6 all-to-all-start
  73.0 115.9 %all-to-all-done = bf16[16,96,1024]{2,1,0:T(8,128)(2,1)} async-done(((bf16[16,96,1024]{2,1,0:T(8,128)(2,1)}), bf16[16,96,1024]{2,1,0:T(8,128)(2,1)}, u32[]{:S(2)}, u32[]{:S(2)}) %all-to-all-start) | async-done | bytes 3145760 | tf_op jit(solution)/shard_map/all_to_all | solution.py:152
  201.8 4.4 copy.128
  207.8 278.0 %while.47 = (s32[]{:T(128)}, f32[2,273,64]{1,2,0:T(8,128)S(1)}, f32[2,273]{1,0:T(2,128)S(1)}, s32[]{:T(128)}, bf16[16,2,512,64]{2,3,1,0:T(8,128)(2,1)}, /*index=...) while((s32[]{:T(128)}, f32[2,273,64]{1,2,0:T(8,128)S(1)}, ...), condition=%wide.region_4.5_spmd.clone, body=%wide.region_1.4_spmd.clone.sunk | while | flops 477021408 | bytes 14363353 | solution.py:84
  485.8 4.2 copy.130
  490.0 4.1 convert_element_type.212
  494.1 4.2 copy.131
  498.2 5.5 all-to-all-start.1
  503.8 41.4 %all-gather.1 = bf16[8,1,128]{2,1,0:T(2,128)(2,1)S(1)} all-gather(bf16[1,1,128]{2,1,0:T(2,128)(2,1)S(1)} %bitcast.362), channel_id=1, replica_groups=mesh['dp'=4,'sp'=8] {'sp'}, dimensions={0}, use_global_device_ids=true | all-gather | bytes 2304 | tf_op jit(solution)/shard_map/all_gather | solution.py:139
  545.2 4.4 copy.133
  553.0 4.8 multiply_reduce_fusion.6
  561.5 11.3 fusion.89
  572.8 11.3 fusion.88
  584.1 20.1 %multiply_convert_fusion = (bf16[1024,2752]{0,1:T(8,128)(2,1)}, bf16[1024,2752]{0,1:T(8,128)(2,1)}, bf16[1024,2752]{0,1:T(8,128)(2,1)}) fusion(f32[1024,2752]{0,1:T(8,128)} %fusion.88, f32[1024,2752]{0,1:T(8,128)} %fusion.89, bf16[1024,1024]{1,0:T(8,128)(2,1)S(1)} %copy-done.9, bf16[2752,1024]{1,0:T(8,128)(2,1)} %all-gather.16.cloned.1.call-done), kind=kOutput, calls=%fused_computation.130 | convolution fusion | flops 5816451072 | bytes 47185920 | tf_op jit(solution)/shard_map/dot_general | solution.py:206
  604.2 11.5 fusion.87
  615.7 10.2 multiply_reduce_fusion.4
  629.0 5.3 convolution_convert_fusion.6
  638.3 10.8 convolution_convert_fusion
  649.1 8.3 copy.183
  659.1 10.5 convolution_convert_fusion.2
  669.6 8.3 copy.179
  679.5 5.9 convolution_convert_fusion.5
  685.3 10.1 all-to-all-start.2
  695.6 10.3 convolution_convert_fusion.1
  705.8 8.4 copy.181
  714.3 64.4 %all-to-all-done.2 = bf16[8,128,1024]{2,1,0:T(8,128)(2,1)S(1)} async-done(((bf16[8,128,1024]{2,1,0:T(8,128)(2,1)}), bf16[8,128,1024]{2,1,0:T(8,128)(2,1)S(1)}, u32[]{:S(2)}, u32[]{:S(2)}) %all-to-all-start.2) | async-done | bytes 2097184 | tf_op jit(solution)/shard_map/all_to_all | solution.py:232
  779.2 4.4 copy.136
  783.6 5.0 reshape.355
  790.2 394.0 %while.48 = (s32[]{:T(128)}, f32[2,273,64]{1,2,0:T(8,128)S(1)}, f32[2,273]{1,0:T(2,128)S(1)}, bf16[16,2,512,16]{2,3,1,0:T(8,128)(2,1)S(1)}, bf16[16,2,512,16]{2,...) while((s32[]{:T(128)}, f32[2,273,64]{1,2,0:T(8,128)S(1)}, ...), condition=%wide.region_14.15_spmd.clone, body=%wide.region_7.14_spmd.clone.sunk | while | flops 1318872064 | bytes 42693776 | solution.py:84
  1186.3 7.0 copy.144
  1193.3 98.5 %all_to_all.53 = bf16[2,96,8192]{1,0,2:T(2,128)(2,1)} all-to-all(bf16[2,96,8192]{1,0,2:T(2,128)(2,1)} %copy.144), channel_id=1, replica_groups=mesh['dp'=4,'sp'=8] {'sp'}, dimensions={2} | all-to-all | bytes 6291456 | tf_op jit(solution)/shard_map/all_to_all | solution.py:237
  1291.8 11.0 copy.174
  1302.8 6.0 convolution_convert_fusion.4
  1315.9 3.9 copy.153
  1330.3 11.2 reduce-scatter.16.cloned.1.call-done
  1341.5 32.1 %reduce-scatter.18.cloned.1.call-done = bf16[128,256]{1,0:T(8,128)(2,1)} async-done(((bf16[1024,256]{1,0:T(8,128)(2,1)}), bf16[128,256]{1,0:T(8,128)(2,1)}) %reduce-scatter.18.cloned.1.call-update) | async-done | bytes 65552 | tf_op jit(solution)/shard_map/reduce_scatter | solution.py:259
  1373.6 36.8 %reduce-scatter.20.cloned.1.call-done = bf16[128,1024]{1,0:T(8,128)(2,1)} async-done(((bf16[1024,1024]{1,0:T(8,128)(2,1)}), bf16[128,1024]{1,0:T(8,128)(2,1)}) %reduce-scatter.20.cloned.1.call-update) | async-done | bytes 262160 | tf_op jit(solution)/shard_map/reduce_scatter | solution.py:262
  1410.5 11.5 add_convert_fusion
  1425.9 9.1 fusion.70
  1434.9 14.8 all-reduce.2
  1449.8 9.8 all-reduce.3
  1460.6 6.9 fusion.72
  1467.5 5.3 copy.155
  1472.9 23.2 %all-reduce.7.cloned.1.call-done = (bf16[128,256]{1,0:T(8,128)(2,1)}, bf16[128,256]{1,0:T(8,128)(2,1)}, bf16[128,1024]{1,0:T(8,128)(2,1)}, bf16[1024,128]{1,0:T(...) async-done(((bf16[128,256]{1,0:T(8,128)(2,1)}, bf16[128,256]{1,0:T(8,128)(2,1)}, bf16[128,1024]{1,0:T(8,128)(2,1)}, ...) | async-done | bytes 2768912 | tf_op jit(solution)/shard_map/psum | solution.py:283
  (1273 shorter events, 702.2 us)
Async XLA Ops:
  7.2 51.7 %all-gather.8.cloned.1.call-start = ((), (), s32[]{:S(2)}) async-start(), calls=%async_computation.11 | async-start | bytes 2359296 | tf_op jit(solution)/shard_map/all_gather | solution.py:135
  9.0 540.6 %all-gather.10.cloned.1.call-start = ((), (), s32[]{:S(2)}) async-start(), calls=%async_computation.12 | async-start | bytes 2359296 | tf_op jit(solution)/shard_map/all_gather | solution.py:136
  9.8 550.5 %all-gather.14.cloned.1.call-start = ((), (), s32[]{:S(2)}) async-start(), calls=%async_computation.14 | async-start | bytes 6340608 | tf_op jit(solution)/shard_map/all_gather | solution.py:141
  10.5 562.3 %all-gather.12.cloned.1.call-start = ((), (), s32[]{:S(2)}) async-start(), calls=%async_computation.13 | async-start | bytes 6340608 | tf_op jit(solution)/shard_map/all_gather | solution.py:140
  11.1 16.4 %copy-start.22 = (bf16[128,256]{1,0:T(8,128)(2,1)S(1)}, bf16[128,256]{1,0:T(8,128)(2,1)}, u32[]{:S(2)}) copy-start(bf16[128,256]{1,0:T(8,128)(2,1)} %param.19) | copy-start | bytes 196612
  11.1 16.5 %copy-start.23 = (bf16[128,256]{1,0:T(8,128)(2,1)S(1)}, bf16[128,256]{1,0:T(8,128)(2,1)}, u32[]{:S(2)}) copy-start(bf16[128,256]{1,0:T(8,128)(2,1)} %param.20) | copy-start | bytes 196612
  14.0 538.9 %copy-start = (bf16[1024,1024]{0,1:T(8,128)(2,1)}, bf16[1024,1024]{0,1:T(8,128)(2,1)S(1)}, u32[]{:S(2)}) copy-start(bf16[1024,1024]{0,1:T(8,128)(2,1)S(1)} %copy.122) | copy-start | bytes 6291460
  27.5 33.4 %copy-start.27 = (f32[8,1,128]{2,1,0:T(1,128)}, f32[8,1,128]{2,1,0:T(1,128)S(1)}, u32[]{:S(2)}) copy-start(f32[8,1,128]{2,1,0:T(1,128)S(1)} %convert_element_type.246) | copy-start | bytes 12292
  28.8 32.0 %copy-start.29 = (f32[1024]{0:T(1024)}, f32[1024]{0:T(1024)S(1)}, u32[]{:S(2)}) copy-start(f32[1024]{0:T(1024)S(1)} %fusion.80) | copy-start | bytes 12292
  60.9 5.0 copy-start.7
  65.9 5.7 copy-start.26
  65.9 123.0 %all-to-all-start = ((bf16[16,96,1024]{2,1,0:T(8,128)(2,1)}), bf16[16,96,1024]{2,1,0:T(8,128)(2,1)}, u32[]{:S(2)}, u32[]{:S(2)}) async-start(bf16[16,96,1024]{2,1,0:T(8,128)(2,1)} %bitcast.333), calls=%async_computation | async-start | bytes 6291456 | tf_op jit(solution)/shard_map/all_to_all | solution.py:152
  70.5 513.7 %all-gather.16.cloned.1.call-start = ((), (), s32[]{:S(2)}) async-start(), calls=%async_computation.15 | async-start | bytes 6340608 | tf_op jit(solution)/shard_map/all_gather | solution.py:142
  219.2 4.9 copy-start.36
  236.5 4.9 copy-start.36
  253.9 4.8 copy-start.36
  271.3 4.8 copy-start.36
  288.7 4.8 copy-start.36
  306.0 4.8 copy-start.36
  340.8 4.8 copy-start.36
  358.1 4.8 copy-start.36
  375.5 4.8 copy-start.36
  392.8 4.9 copy-start.36
  410.2 4.9 copy-start.36
  427.6 4.9 copy-start.36
  444.9 4.8 copy-start.36
  462.3 4.9 copy-start.36
  479.7 4.8 copy-start.36
  498.2 5.6 copy-start.33
  498.2 54.7 %all-to-all-start.1 = ((bf16[128,8,1024]{2,0,1:T(8,128)(2,1)}), bf16[128,8,1024]{2,0,1:T(8,128)(2,1)}, u32[]{:S(2)}, u32[]{:S(2)}) async-start(bf16[128,8,1024]{2,0,1:T(8,128)(2,1)} %copy.131), calls=%async_computation.1 | async-start | bytes 4194304 | tf_op jit(solution)/shard_map/all_to_all | solution.py:172
  503.8 818.0 %reduce-scatter.22.cloned.1.call-start = ((), (), s32[]{:S(2)}) async-start(), calls=%async_computation.19 | async-start | bytes 2359296
  572.8 11.3 copy-start.9
  604.2 11.5 copy-start.3
  604.2 11.5 copy-start.39
  615.7 10.2 copy-start.5
  638.3 685.3 %reduce-scatter.28.cloned.1.call-start = ((), (), s32[]{:S(2)}) async-start(), calls=%async_computation.22 | async-start | bytes 6488064
  657.5 668.3 %reduce-scatter.24.cloned.1.call-start = ((), (), s32[]{:S(2)}) async-start(), calls=%async_computation.20 | async-start | bytes 6488064
  685.3 93.3 %all-to-all-start.2 = ((bf16[8,128,1024]{2,1,0:T(8,128)(2,1)}), bf16[8,128,1024]{2,1,0:T(8,128)(2,1)S(1)}, u32[]{:S(2)}, u32[]{:S(2)}) async-start(bf16[8,128,1024]{2,1,0:T(8,128)(2,1)} %bitcast.339), calls=%async_computation.2 | async-start | bytes 4194304 | tf_op jit(solution)/shard_map/all_to_all | solution.py:232
  695.5 632.6 %reduce-scatter.26.cloned.1.call-start = ((), (), s32[]{:S(2)}) async-start(), calls=%async_computation.21 | async-start | bytes 6488064
  714.2 627.3 %reduce-scatter.16.cloned.1.call-start = ((), (), s32[]{:S(2)}) async-start(), calls=%async_computation.16 | async-start | bytes 589824 | tf_op jit(solution)/shard_map/reduce_scatter | solution.py:256
  1291.8 11.0 copy-start.1
  1291.8 11.0 copy-start.28
  1291.8 11.0 copy-start.30
  1311.6 62.0 %reduce-scatter.18.cloned.1.call-start = ((), (), s32[]{:S(2)}) async-start(), calls=%async_computation.17 | async-start | bytes 589824 | tf_op jit(solution)/shard_map/reduce_scatter | solution.py:259
  1312.7 97.7 %reduce-scatter.20.cloned.1.call-start = ((), (), s32[]{:S(2)}) async-start(), calls=%async_computation.18 | async-start | bytes 2359296 | tf_op jit(solution)/shard_map/reduce_scatter | solution.py:262
  1319.9 176.2 %all-reduce.7.cloned.1.call-start = ((), (), s32[]{:S(2)}) async-start(), calls=%async_computation.23 | async-start | bytes 5537792 | tf_op jit(solution)/shard_map/psum | solution.py:283
  1425.9 9.1 copy-start.31
  1425.9 34.8 %copy-start.25 = (f32[1024]{0:T(1024)S(1)}, f32[1024]{0:T(1024)}, u32[]{:S(2)}) copy-start(f32[1024]{0:T(1024)} %copy-done.24) | copy-start | bytes 12292
  (113 other events, 213.2 us)
Sparse Core Ops, SparseCore 0:
  10.2 37.7 all-gather.7
  49.5 39.1 all-gather.9
  90.3 103.3 all-gather.13
  195.2 58.0 all-gather.11
  254.8 57.9 all-gather.15
  638.4 42.0 reduce-scatter.21
  682.7 100.5 reduce-scatter.27
  785.6 70.4 reduce-scatter.23
  858.4 63.2 reduce-scatter.25
  1311.8 29.6 reduce-scatter.15
  1344.4 29.1 reduce-scatter.17
  1376.3 34.0 reduce-scatter.19
  1415.0 81.0 all-reduce.6
where the time goes:
time: 1530 us; the launch traced here: 1510 us
  matrix products  473 us (31%)
  waiting for transfers between devices  289 us (19%)
  local copies, waits for them, and re-layouts  286 us (19%)
  blocking collectives  208 us (14%)
  other arithmetic  170 us (11%)
  loops' own time  48 us (3%)
  starting transfers between devices  20.9 us (1%)
  between operations  15.3 us (1%)
    dot_general x64, matrix products, attend_block(): jnp.einsum('hij,hjv->hiv', weights, value_blk, precision=CAREFUL)  118 us
    all_to_all x1, waiting for transfers between devices, body(): lax.all_to_all(projected.reshape(head_count, per_head, tok_local), 'sp',...  116 us
    all_to_all x1, blocking collectives, body(): lax.all_to_all(grad_stack, 'sp', split_axis=2, concat_axis=0, tiled=True)  98.5 us
    unnamed x91, local copies, waits for them, and re-layouts  80.6 us
    dot_general x64, matrix products, attend_block(): scores = jnp.einsum('hif,hjf->hij', query_blk, key_blk, precision=CAREFUL)  75.8 us
    all_to_all x1, waiting for transfers between devices, body(): lax.all_to_all(grad_attended, 'sp', split_axis=0, concat_axis=1, tiled=True)  64.4 us
    squeeze x64, local copies, waits for them, and re-layouts, attend(): lax.scan(jax.checkpoint(attend_block), initial, (blocked(queries), blocke...  56.3 us
    dynamic_slice x48, local copies, waits for them, and re-layouts, attend(): lax.scan(jax.checkpoint(attend_block), initial, (blocked(queries), blocke...  50.9 us
  transfers between devices with their start and end apart: 16, of which 7 were waited for; matrix products, arithmetic and copies ran while one was open for 56% of the time, Pallas kernels for 0%

commit v1 on v0

--- a/solution.py
+++ b/solution.py
@@ -3,12 +3,36 @@
 import jax.numpy as jnp
 from jax import lax
 from jax.sharding import PartitionSpec as P
+from jax.lax import axis_index, axis_size, ppermute
 
 FEAT = 16
 HEAD_V = 64
 BLOCK = 512
 EPSILON = 1e-05
 CAREFUL = lax.Precision.HIGH
+
+
+def lots_all_part(page, in_dim):
+    w_next, y1, small = (axis_size("sp"), axis_index("sp"), page.shape[in_dim])
+    shelf = []
+    for m in range(w_next):
+        shelf.append((m, (m + 1) % w_next))
+    store = []
+    for m in range(w_next):
+        store.append((m, (m - 1) % w_next))
+    o_now = jnp.zeros((*page.shape[:in_dim], w_next * small, *page.shape[in_dim + 1 :]), page.dtype)
+    o_now = lax.dynamic_update_slice_in_dim(o_now, page, y1 * small, axis=in_dim)
+    val = right_arr = page
+    x_next = w_next // 2
+    for i in range(1, x_next + 1):
+        val = ppermute(val, axis_name="sp", perm=shelf)
+        o_now = lax.dynamic_update_slice_in_dim(o_now, val, (y1 - i) % w_next * small, axis=in_dim)
+        if i < w_next - x_next:
+            right_arr = ppermute(right_arr, axis_name="sp", perm=store)
+            o_now = lax.dynamic_update_slice_in_dim(
+                o_now, right_arr, (y1 + i) % w_next * small, axis=in_dim
+            )
+    return o_now
 
 
 def rms_scale(values, weights):
@@ -136,7 +160,7 @@
         lax.all_gather(w_out, "sp", axis=1, tiled=True),
     )
     mlp_full = (
-        lax.all_gather(gain_mlp, "sp", axis=0, tiled=True),
+        lots_all_part(gain_mlp, 0),
         lax.all_gather(w_gate, "sp", axis=0, tiled=True),
         lax.all_gather(w_up, "sp", axis=0, tiled=True),
         lax.all_gather(w_down, "sp", axis=1, tiled=True),

time: 1530 us -> 1510 us (0.987)
  blocking collectives: 208 us -> 167 us
  waiting for transfers between devices: 289 us -> 310 us
    all_gather x1 -> x0, blocking collectives: 41.4 us -> none  [body(): lax.all_gather(gain_mlp, 'sp', axis=0, tiled=True)]
    ppermute x0 -> x7, waiting for transfers between devices: none -> 34.7 us  [the longest x4 34.7 us: lots_all_part(): val = ppermute(val, axis_name='sp', perm=shelf)]
  transfers between devices with their start and end apart: 16 -> 23, of which waited for: 7 -> 10; matrix products, arithmetic and copies ran while one was open for 56% -> 57% of each run, Pallas kernels for 0% -> 0%
where the time goes in v1:
time: 1510 us; the launch traced here: 1500 us
  matrix products  472 us (31%)
  waiting for transfers between devices  310 us (21%)
  local copies, waits for them, and re-layouts  286 us (19%)
  other arithmetic  170 us (11%)
  blocking collectives  167 us (11%)
  loops' own time  47.7 us (3%)
  starting transfers between devices  29.2 us (2%)
  between operations  15.3 us (1%)
    dot_general x64, matrix products, attend_block(): jnp.einsum('hij,hjv->hiv', weights, value_blk, precision=CAREFUL)  118 us
    all_to_all x1, waiting for transfers between devices, body(): lax.all_to_all(projected.reshape(head_count, per_head, tok_local), 'sp',...  106 us
    all_to_all x1, blocking collectives, body(): lax.all_to_all(grad_stack, 'sp', split_axis=2, concat_axis=0, tiled=True)  98.5 us
    unnamed x91, local copies, waits for them, and re-layouts  79.4 us
    dot_general x64, matrix products, attend_block(): scores = jnp.einsum('hif,hjf->hij', query_blk, key_blk, precision=CAREFUL)  75.9 us
    all_to_all x1, waiting for transfers between devices, body(): lax.all_to_all(grad_attended, 'sp', split_axis=0, concat_axis=1, tiled=True)  63.8 us
    squeeze x64, local copies, waits for them, and re-layouts, attend(): lax.scan(jax.checkpoint(attend_block), initial, (blocked(queries), blocke...  56.3 us
    dynamic_slice x48, local copies, waits for them, and re-layouts, attend(): lax.scan(jax.checkpoint(attend_block), initial, (blocked(queries), blocke...  51.4 us
  transfers between devices with their start and end apart: 23, of which 10 were waited for; matrix products, arithmetic and copies ran while one was open for 57% of the time, Pallas kernels for 0%

profile of v1, /device:TPU:0, one launch (start us, length us, event | category | flops | bytes accessed | tf_op | source)
XLA Modules:
  0.0 1496.8 jit_solution(7760946045770398091)
XLA Ops:
  14.1 13.4 all-gather
  28.8 16.1 %all_gather.31 = bf16[1024,256]{0,1:T(8,128)(2,1)S(1)} all-gather(bf16[128,256]{0,1:T(8,128)(2,1)S(1)} %copy.123), channel_id=1, replica_groups=mesh['dp'=4,'sp'=8] {'sp'}, dimensions={0}, use_global_device_ids=true | all-gather | bytes 589824 | tf_op jit(solution)/shard_map/all_gather | solution.py:157
  45.0 13.9 all_gather.32
  60.9 5.0 convolution_convert_fusion.3
  65.9 4.6 all-to-all-start
  73.0 106.1 %all-to-all-done = bf16[16,96,1024]{2,1,0:T(8,128)(2,1)} async-done(((bf16[16,96,1024]{2,1,0:T(8,128)(2,1)}), bf16[16,96,1024]{2,1,0:T(8,128)(2,1)}, u32[]{:S(2)}, u32[]{:S(2)}) %all-to-all-start) | async-done | bytes 3145760 | tf_op jit(solution)/shard_map/all_to_all | solution.py:176
  192.0 4.4 copy.128
  198.0 276.6 %while.47 = (s32[]{:T(128)}, f32[2,273,64]{1,2,0:T(8,128)S(1)}, f32[2,273]{1,0:T(2,128)S(1)}, s32[]{:T(128)}, bf16[16,2,512,64]{2,3,1,0:T(8,128)(2,1)}, /*index=...) while((s32[]{:T(128)}, f32[2,273,64]{1,2,0:T(8,128)S(1)}, ...), condition=%wide.region_4.5_spmd.clone, body=%wide.region_1.4_spmd.clone.sunk | while | flops 477021408 | bytes 14363353 | solution.py:108
  474.6 4.2 copy.130
  478.7 4.1 convert_element_type.212
  482.8 4.1 copy.131
  486.9 4.5 all-to-all-start.1
  499.1 30.5 %collective-permute-done = bf16[128]{0:T(256)(128)(2,1)S(1)} collective-permute-done((bf16[128]{0:T(256)(128)(2,1)S(1)}, bf16[128]{0:T(256)(128)(2,1)S(1)}, u32[]{:S(2)}, u32[]{:S(2)}) %collective-permute-start) | collective-permute-done | bytes 288 | tf_op jit(solution)/shard_map/ppermute | solution.py:28
  544.1 11.2 fusion.87
  555.3 4.8 multiply_reduce_fusion.6
  562.6 12.0 fusion.89
  574.6 20.4 %multiply_convert_fusion = (bf16[1024,2752]{0,1:T(8,128)(2,1)}, bf16[1024,2752]{0,1:T(8,128)(2,1)}, bf16[1024,2752]{0,1:T(8,128)(2,1)}) fusion(f32[1024,2752]{0,1:T(8,128)} %fusion.87, f32[1024,2752]{0,1:T(8,128)} %fusion.89, bf16[1024,2752]{0,1:T(8,128)(2,1)} %all-gather.11.cloned.1.call-done, bf16[1024,1024]{0,1:T(8,128)(2,1)S(1)} %multiply_convert_fusion.3), kind=kOutput, calls=%fused_computation.130 | convolution fusion | flops 5816451072 | bytes 47185920 | tf_op jit(solution)/shard_map/dot_general | solution.py:203
  595.0 11.3 fusion.88
  606.3 10.3 multiply_reduce_fusion.4
  619.7 4.0 convolution_convert_fusion.6
  628.2 10.4 convolution_convert_fusion
  638.6 8.3 copy.183
  648.5 10.5 convolution_convert_fusion.1
  659.0 8.3 copy.181
  669.0 5.8 convolution_convert_fusion.5
  674.8 7.3 all-to-all-start.2
  682.2 10.3 convolution_convert_fusion.2
  692.5 8.3 copy.179
  700.9 63.8 %all-to-all-done.2 = bf16[8,128,1024]{2,1,0:T(8,128)(2,1)S(1)} async-done(((bf16[8,128,1024]{2,1,0:T(8,128)(2,1)}), bf16[8,128,1024]{2,1,0:T(8,128)(2,1)S(1)}, u32[]{:S(2)}, u32[]{:S(2)}) %all-to-all-start.2) | async-done | bytes 2097184 | tf_op jit(solution)/shard_map/all_to_all | solution.py:256
  765.2 4.4 copy.136
  769.6 5.0 reshape.355
  776.3 394.1 %while.48 = (s32[]{:T(128)}, f32[2,273,64]{1,2,0:T(8,128)S(1)}, f32[2,273]{1,0:T(2,128)S(1)}, bf16[16,2,512,16]{2,3,1,0:T(8,128)(2,1)S(1)}, bf16[16,2,512,16]{2,...) while((s32[]{:T(128)}, f32[2,273,64]{1,2,0:T(8,128)S(1)}, ...), condition=%wide.region_14.15_spmd.clone, body=%wide.region_7.14_spmd.clone.sunk | while | flops 1318872064 | bytes 42693776 | solution.py:108
  1172.4 7.0 copy.144
  1179.4 98.5 %all_to_all.53 = bf16[2,96,8192]{1,0,2:T(2,128)(2,1)} all-to-all(bf16[2,96,8192]{1,0,2:T(2,128)(2,1)} %copy.144), channel_id=1, replica_groups=mesh['dp'=4,'sp'=8] {'sp'}, dimensions={2} | all-to-all | bytes 6291456 | tf_op jit(solution)/shard_map/all_to_all | solution.py:261
  1277.9 11.0 copy.174
  1289.0 6.0 convolution_convert_fusion.4
  1302.0 3.9 copy.153
  1316.4 11.2 reduce-scatter.16.cloned.1.call-done
  1327.7 32.1 %reduce-scatter.18.cloned.1.call-done = bf16[128,256]{1,0:T(8,128)(2,1)} async-done(((bf16[1024,256]{1,0:T(8,128)(2,1)}), bf16[128,256]{1,0:T(8,128)(2,1)}) %reduce-scatter.18.cloned.1.call-update) | async-done | bytes 65552 | tf_op jit(solution)/shard_map/reduce_scatter | solution.py:283
  1359.8 36.8 %reduce-scatter.20.cloned.1.call-done = bf16[128,1024]{1,0:T(8,128)(2,1)} async-done(((bf16[1024,1024]{1,0:T(8,128)(2,1)}), bf16[128,1024]{1,0:T(8,128)(2,1)}) %reduce-scatter.20.cloned.1.call-update) | async-done | bytes 262160 | tf_op jit(solution)/shard_map/reduce_scatter | solution.py:286
  1396.6 11.5 add_convert_fusion
  1408.1 3.9 copy.154
  1412.0 9.1 fusion.70
  1421.1 14.7 all-reduce.2
  1436.0 9.8 all-reduce.3
  1446.8 6.9 fusion.72
  1453.8 5.3 copy.155
  1459.1 23.1 %all-reduce.7.cloned.1.call-done = (bf16[128,256]{1,0:T(8,128)(2,1)}, bf16[128,256]{1,0:T(8,128)(2,1)}, bf16[128,1024]{1,0:T(8,128)(2,1)}, bf16[1024,128]{1,0:T(...) async-done(((bf16[128,256]{1,0:T(8,128)(2,1)}, bf16[128,256]{1,0:T(8,128)(2,1)}, bf16[128,1024]{1,0:T(8,128)(2,1)}, ...) | async-done | bytes 2768912 | tf_op jit(solution)/shard_map/psum | solution.py:307
  (1295 shorter events, 715.2 us)
Async XLA Ops:
  7.2 51.8 %all-gather.7.cloned.1.call-start = ((), (), s32[]{:S(2)}) async-start(), calls=%async_computation.11 | async-start | bytes 2359296 | tf_op jit(solution)/shard_map/all_gather | solution.py:159
  9.0 535.1 %all-gather.15.cloned.1.call-start = ((), (), s32[]{:S(2)}) async-start(), calls=%async_computation.15 | async-start | bytes 6340608 | tf_op jit(solution)/shard_map/all_gather | solution.py:166
  9.8 545.5 %all-gather.9.cloned.1.call-start = ((), (), s32[]{:S(2)}) async-start(), calls=%async_computation.12 | async-start | bytes 2359296 | tf_op jit(solution)/shard_map/all_gather | solution.py:160
  10.5 552.0 %all-gather.13.cloned.1.call-start = ((), (), s32[]{:S(2)}) async-start(), calls=%async_computation.14 | async-start | bytes 6340608 | tf_op jit(solution)/shard_map/all_gather | solution.py:165
  11.1 16.4 %copy-start.22 = (bf16[128,256]{1,0:T(8,128)(2,1)S(1)}, bf16[128,256]{1,0:T(8,128)(2,1)}, u32[]{:S(2)}) copy-start(bf16[128,256]{1,0:T(8,128)(2,1)} %param.19) | copy-start | bytes 196612
  11.1 16.5 %copy-start.23 = (bf16[128,256]{1,0:T(8,128)(2,1)S(1)}, bf16[128,256]{1,0:T(8,128)(2,1)}, u32[]{:S(2)}) copy-start(bf16[128,256]{1,0:T(8,128)(2,1)} %param.20) | copy-start | bytes 196612
  14.0 541.3 %copy-start = (bf16[1024,1024]{0,1:T(8,128)(2,1)}, bf16[1024,1024]{0,1:T(8,128)(2,1)S(1)}, u32[]{:S(2)}) copy-start(bf16[1024,1024]{0,1:T(8,128)(2,1)S(1)} %copy.122) | copy-start | bytes 6291460
  27.5 33.4 %copy-start.27 = (f32[8,1,128]{2,1,0:T(1,128)}, f32[8,1,128]{2,1,0:T(1,128)S(1)}, u32[]{:S(2)}) copy-start(f32[8,1,128]{2,1,0:T(1,128)S(1)} %convert_element_type.246) | copy-start | bytes 12292
  28.8 32.1 %copy-start.29 = (f32[1024]{0:T(1024)}, f32[1024]{0:T(1024)S(1)}, u32[]{:S(2)}) copy-start(f32[1024]{0:T(1024)S(1)} %fusion.80) | copy-start | bytes 12292
  60.9 5.0 copy-start.7
  65.9 5.7 copy-start.26
  65.9 113.2 %all-to-all-start = ((bf16[16,96,1024]{2,1,0:T(8,128)(2,1)}), bf16[16,96,1024]{2,1,0:T(8,128)(2,1)}, u32[]{:S(2)}, u32[]{:S(2)}) async-start(bf16[16,96,1024]{2,1,0:T(8,128)(2,1)} %bitcast.331), calls=%async_computation | async-start | bytes 6291456 | tf_op jit(solution)/shard_map/all_to_all | solution.py:176
  70.5 504.1 %all-gather.11.cloned.1.call-start = ((), (), s32[]{:S(2)}) async-start(), calls=%async_computation.13 | async-start | bytes 6340608 | tf_op jit(solution)/shard_map/all_gather | solution.py:164
  209.3 4.9 copy-start.37
  226.6 4.9 copy-start.37
  243.9 4.9 copy-start.37
  261.2 4.8 copy-start.37
  278.4 4.9 copy-start.37
  330.3 4.8 copy-start.37
  364.8 4.9 copy-start.37
  399.4 4.9 copy-start.37
  433.9 4.9 copy-start.37
  486.9 68.4 %all-to-all-start.1 = ((bf16[128,8,1024]{2,0,1:T(8,128)(2,1)}), bf16[128,8,1024]{2,0,1:T(8,128)(2,1)}, u32[]{:S(2)}, u32[]{:S(2)}) async-start(bf16[128,8,1024]{2,0,1:T(8,128)(2,1)} %copy.131), calls=%async_computation.1 | async-start | bytes 4194304 | tf_op jit(solution)/shard_map/all_to_all | solution.py:196
  491.3 816.5 %reduce-scatter.22.cloned.1.call-start = ((), (), s32[]{:S(2)}) async-start(), calls=%async_computation.19 | async-start | bytes 2359296
  491.4 38.2 %collective-permute-start = (bf16[128]{0:T(256)(128)(2,1)S(1)}, bf16[128]{0:T(256)(128)(2,1)S(1)}, u32[]{:S(2)}, u32[]{:S(2)}) collective-permute-start(bf16[128]{0:T(256)(128)(2,1)S(1)} %copy-done.35), channel_id=1, source_target_pairs={{0,1},{1,2},{2,3},{3,4},{4,5},{5,6},{6,7},{7,0},{8,9},{9,10},{10,1... | collective-permute-start | bytes 776 | tf_op jit(solution)/shard_map/ppermute | solution.py:28
  491.8 37.8 %collective-permute-start.1 = (bf16[128]{0:T(256)(128)(2,1)S(1)}, bf16[128]{0:T(256)(128)(2,1)S(1)}, u32[]{:S(2)}, u32[]{:S(2)}) collective-permute-start(bf16[128]{0:T(256)(128)(2,1)S(1)} %copy-done.35), channel_id=1, source_target_pairs={{0,7},{1,0},{2,1},{3,2},{4,3},{5,4},{6,5},{7,6},{8,15},{9,8},{10,9... | collective-permute-start | bytes 776 | tf_op jit(solution)/shard_map/ppermute | solution.py:31
  529.6 4.8 collective-permute-start.2
  529.6 5.1 collective-permute-start.3
  534.4 4.8 collective-permute-start.4
  534.8 6.8 collective-permute-start.5
  539.2 4.8 collective-permute-start.6
  562.5 12.1 copy-start.10
  595.0 11.3 copy-start.3
  595.0 11.3 copy-start.33
  606.3 10.3 copy-start.5
  626.7 683.0 %reduce-scatter.28.cloned.1.call-start = ((), (), s32[]{:S(2)}) async-start(), calls=%async_computation.22 | async-start | bytes 6488064
  647.0 665.0 %reduce-scatter.26.cloned.1.call-start = ((), (), s32[]{:S(2)}) async-start(), calls=%async_computation.21 | async-start | bytes 6488064
  674.8 89.9 %all-to-all-start.2 = ((bf16[8,128,1024]{2,1,0:T(8,128)(2,1)}), bf16[8,128,1024]{2,1,0:T(8,128)(2,1)S(1)}, u32[]{:S(2)}, u32[]{:S(2)}) async-start(bf16[8,128,1024]{2,1,0:T(8,128)(2,1)} %bitcast.337), calls=%async_computation.2 | async-start | bytes 4194304 | tf_op jit(solution)/shard_map/all_to_all | solution.py:256
  682.1 632.0 %reduce-scatter.24.cloned.1.call-start = ((), (), s32[]{:S(2)}) async-start(), calls=%async_computation.20 | async-start | bytes 6488064
  700.9 626.8 %reduce-scatter.16.cloned.1.call-start = ((), (), s32[]{:S(2)}) async-start(), calls=%async_computation.16 | async-start | bytes 589824 | tf_op jit(solution)/shard_map/reduce_scatter | solution.py:280
  1277.9 11.1 copy-start.1
  1277.9 11.1 copy-start.28
  1277.9 11.1 copy-start.30
  1297.8 62.0 %reduce-scatter.18.cloned.1.call-start = ((), (), s32[]{:S(2)}) async-start(), calls=%async_computation.17 | async-start | bytes 589824 | tf_op jit(solution)/shard_map/reduce_scatter | solution.py:283
  1298.8 97.8 %reduce-scatter.20.cloned.1.call-start = ((), (), s32[]{:S(2)}) async-start(), calls=%async_computation.18 | async-start | bytes 2359296 | tf_op jit(solution)/shard_map/reduce_scatter | solution.py:286
  1306.0 176.2 %all-reduce.7.cloned.1.call-start = ((), (), s32[]{:S(2)}) async-start(), calls=%async_computation.23 | async-start | bytes 5537792 | tf_op jit(solution)/shard_map/psum | solution.py:307
  1412.0 9.1 copy-start.31
  1412.0 34.8 %copy-start.25 = (f32[1024]{0:T(1024)S(1)}, f32[1024]{0:T(1024)}, u32[]{:S(2)}) copy-start(f32[1024]{0:T(1024)} %copy-done.24) | copy-start | bytes 12292
  (120 other events, 245.8 us)
Sparse Core Ops, SparseCore 0:
  10.2 37.7 all-gather.6
  49.5 112.0 all-gather.14
  163.2 29.9 all-gather.8
  194.6 62.4 all-gather.12
  258.5 59.5 all-gather.10
  626.8 38.9 reduce-scatter.21
  668.1 99.4 reduce-scatter.27
  769.8 71.8 reduce-scatter.25
  844.0 63.1 reduce-scatter.23
  1297.9 29.7 reduce-scatter.15
  1330.6 29.1 reduce-scatter.17
  1362.5 34.0 reduce-scatter.19
  1401.1 81.0 all-reduce.6
